TPU v7x, 512 devices: a whole 4x8x8 slice. The times are simulated.
512 devices in a mesh: ctx: 64 (over x, y_lo, z), tp: 8 (over y_hi, core).
Axes of the slice: x: 4, y: 8 (y_hi: 4, y_lo: 2; y = y_hi * 2 + y_lo), z: 8, core: 2. Of those that a mesh axis runs over, the one named last changes fastest.
Arguments:
- query_vectors: bfloat16 [8192, 3072], P(('ctx', 'tp')), may hold values from -20 to 20
- key_vectors: bfloat16 [8192, 3072], P(('ctx', 'tp')), may hold values from -20 to 20
- value_vectors: bfloat16 [8192, 3072], P(('ctx', 'tp')), may hold values from -6 to 6
- out_weight: bfloat16 [3072, 5120], P('tp'), may hold values from -0.109375 to 0.109375
Outputs:
- mixed: bfloat16 [8192, 5120], P(('ctx', 'tp'))
All inputs are finite; a program needn't handle non-finite values.
Results may differ from a plain program's by a relative error of at most 0.027.
Values may be sent and summed in bfloat16 or wider, within the bound.
A program may use at most 64 MiB of HBM per device.

v0:
```python
import math
import jax
import jax.numpy as jnp
from jax import lax
from jax.sharding import PartitionSpec as P

HD = 128


def fresh_state(row_count, head_count):
    row_peak = jnp.full((row_count, head_count), -1e30, jnp.float32)
    row_total = jnp.zeros((row_count, head_count), jnp.float32)
    weighted = jnp.zeros((row_count, head_count, HD), jnp.float32)
    return (row_peak, row_total, weighted)


def attend_piece(running, query_heads, key_rows, value_rows, score_scale):
    head_count = query_heads.shape[1]
    piece_rows = key_rows.shape[0]
    sub_rows = math.gcd(piece_rows, 256)
    sub_count = piece_rows // sub_rows
    key_parts = key_rows.reshape(sub_count, sub_rows, head_count, HD)
    value_parts = value_rows.reshape(sub_count, sub_rows, head_count, HD)

    def absorb(current, part_pair):
        row_peak, row_total, weighted = current
        key_part, value_part = part_pair
        scores = (
            jnp.einsum("ihd,jhd->ihj", query_heads, key_part, preferred_element_type=jnp.float32)
            * score_scale
        )
        new_peak = jnp.maximum(row_peak, jnp.max(scores, axis=-1))
        weights_low = jnp.exp(scores - new_peak[..., None]).astype(jnp.bfloat16)
        shrink = jnp.exp(row_peak - new_peak)
        row_total = row_total * shrink + jnp.sum(weights_low.astype(jnp.float32), axis=-1)
        weighted = weighted * shrink[..., None] + jnp.einsum(
            "ihj,jhd->ihd", weights_low, value_part, preferred_element_type=jnp.float32
        )
        return ((new_peak, row_total, weighted), None)

    finished, unused = lax.scan(absorb, running, (key_parts, value_parts))
    return finished


def local(query_vectors, key_vectors, value_vectors, out_weight):
    score_scale = 1.0 / math.sqrt(HD)
    tp_count = lax.axis_size("tp")
    all_queries = lax.all_gather(query_vectors, "tp", axis=0, tiled=True)
    row_count = all_queries.shape[0]
    head_count = all_queries.shape[1] // HD
    query_heads = all_queries.reshape(row_count, head_count, HD)
    row_peak, row_total, weighted = attend_piece(
        fresh_state(row_count, head_count),
        query_heads,
        lax.all_gather(key_vectors, "ctx", axis=0, tiled=True),
        lax.all_gather(value_vectors, "ctx", axis=0, tiled=True),
        score_scale,
    )
    top_peak = lax.pmax(row_peak, "tp")
    factor = jnp.exp(row_peak - top_peak)
    all_totals = lax.psum(row_total * factor, "tp")
    numerator = (weighted * factor[..., None]).reshape(row_count, head_count * HD)
    own_numerator = lax.psum_scatter(
        numerator.astype(jnp.bfloat16), "tp", scatter_dimension=1, tiled=True
    ).astype(jnp.float32)
    own_heads = head_count // tp_count
    own_totals = lax.dynamic_slice_in_dim(
        all_totals, lax.axis_index("tp") * own_heads, own_heads, 1
    )
    attended = (own_numerator.reshape(row_count, own_heads, HD) / own_totals[..., None]).astype(
        jnp.bfloat16
    )
    attended = attended.reshape(row_count, own_heads * HD)
    return lax.psum_scatter(
        jnp.dot(attended, out_weight, preferred_element_type=jnp.float32).astype(jnp.bfloat16),
        "tp",
        scatter_dimension=0,
        tiled=True,
    )


def solution(mesh):
    return jax.shard_map(
        local,
        mesh=mesh,
        in_specs=(
            P(("ctx", "tp"), None),
            P(("ctx", "tp"), None),
            P(("ctx", "tp"), None),
            P("tp", None),
        ),
        out_specs=P(("ctx", "tp"), None),
        check_vma=False,
    )
```

profile of v0, /device:TPU:21, one launch (start us, length us, event | category | flops | bytes accessed | tf_op | source)
XLA Modules:
  0.0 811.8 jit_solution(7666811695530442042)
XLA Ops:
  6.5 0.0 all-gather.5.cloned.1.call-start
  6.5 0.7 all-gather.5.cloned.1.call-update
  7.3 0.0 all-gather.3.cloned.1.call-start
  7.3 0.7 all-gather.3.cloned.1.call-update
  8.0 0.0 reduce-scatter.3.cloned.1.call-start
  8.1 17.3 %all_gather.10 = bf16[128,3072]{1,0:T(8,128)(2,1)S(1)} all-gather(bf16[16,3072]{1,0:T(8,128)(2,1)} %param.6), channel_id=1, replica_groups=mesh['ctx'=64,'tp'=8] {'tp'}, dimensions={0}, use_global_device_ids=true | all-gather | bytes 884736 | tf_op jit(solution)/shard_map/all_gather | solution.py:48
  25.4 0.4 copy.12
  25.8 1.2 copy.14
  27.0 224.2 %all-gather.5.cloned.1.call-done = bf16[1024,3072]{1,0:T(8,128)(2,1)} async-done(((bf16[16,3072]{1,0:T(8,128)(2,1)}), bf16[1024,3072]{1,0:T(8,128)(2,1)}) %all-gather.5.cloned.1.call-update) | async-done | bytes 6291472 | tf_op jit(solution)/shard_map/all_gather | solution.py:56
  251.1 7.4 copy.20
  258.5 303.4 %all-gather.3.cloned.1.call-done = bf16[1024,3072]{1,0:T(8,128)(2,1)} async-done(((bf16[16,3072]{1,0:T(8,128)(2,1)}), bf16[1024,3072]{1,0:T(8,128)(2,1)}) %all-gather.3.cloned.1.call-update) | async-done | bytes 6291472 | tf_op jit(solution)/shard_map/all_gather | solution.py:55
  562.0 7.4 copy.19
  569.4 46.2 %while.15 = (s32[]{:T(128)}, f32[128,24]{0,1:T(8,128)S(1)}, f32[128,24]{0,1:T(8,128)S(1)}, f32[128,24,128]{0,2,1:T(8,128)}, bf16[4,256,24,128]{3,2,1,0:T(8,128)(...) while((s32[]{:T(128)}, f32[128,24]{0,1:T(8,128)S(1)}, ...), condition=%wide.region_3.4_spmd.clone, body=%wide.region_0.3_spmd.clone.sunk | while | flops 411712512 | bytes 29294728 | solution.py:41
  569.4 0.0 copy-start
  569.4 3.6 constant_dynamic-slice_fusion.4
  573.0 0.0 copy-done
  573.0 0.6 bitcast_reduce_fusion.2
  573.6 0.5 convert_reduce_fusion.2
  574.2 2.9 copy.28
  577.1 3.5 bitcast_add_fusion.2
  580.6 3.6 constant_dynamic-slice_fusion.4
  584.2 0.0 copy-done
  584.2 0.6 bitcast_reduce_fusion.2
  584.8 0.5 convert_reduce_fusion.2
  585.4 2.9 copy.28
  588.3 4.0 bitcast_add_fusion.2
  592.2 3.6 constant_dynamic-slice_fusion.4
  595.9 0.0 copy-done
  595.9 0.6 bitcast_reduce_fusion.2
  596.5 0.5 convert_reduce_fusion.2
  597.1 2.9 copy.28
  599.9 3.9 bitcast_add_fusion.2
  603.9 3.6 constant_dynamic-slice_fusion.4
  607.5 0.0 copy-done
  607.5 0.6 bitcast_reduce_fusion.2
  608.2 0.5 convert_reduce_fusion.2
  608.7 2.9 copy.28
  611.6 3.9 bitcast_add_fusion.2
  615.6 66.1 %pmax.7 = f32[128,24]{0,1:T(8,128)S(1)} all-reduce(f32[128,24]{0,1:T(8,128)S(1)} %get-tuple-element.45), channel_id=1, replica_groups=mesh['ctx'=64,'tp'=8] {'tp'}, use_global_device_ids=true, to_apply=%region_4.5 | all-reduce | flops 3072 | bytes 24576 | tf_op jit(solution)/shard_map/pmax | solution.py:59
  681.7 2.5 multiply_convert_fusion
  684.2 0.0 reduce-scatter.3.cloned.1.call-update
  684.2 0.0 reduce-scatter.5.cloned.1.call-start
  684.3 27.2 %psum.7 = f32[128,24]{0,1:T(8,128)S(1)} all-reduce(f32[128,24]{0,1:T(8,128)S(1)} %get-tuple-element.101), channel_id=1, replica_groups=mesh['ctx'=64,'tp'=8] {'tp'}, use_global_device_ids=true, to_apply=%region_6.7 | all-reduce | flops 3072 | bytes 24576 | tf_op jit(solution)/shard_map/psum | solution.py:61
  711.5 46.7 %reduce-scatter.3.cloned.1.call-done = bf16[128,384]{0,1:T(8,128)(2,1)} async-done(((bf16[128,3072]{0,1:T(8,128)(2,1)}), bf16[128,384]{0,1:T(8,128)(2,1)}) %reduce-scatter.3.cloned.1.call-update) | async-done | bytes 98320 | tf_op jit(solution)/shard_map/reduce_scatter | solution.py:63
  758.2 0.9 fusion.10
  759.1 4.1 convolution_convert_fusion
  763.2 0.0 reduce-scatter.5.cloned.1.call-update
  763.2 42.1 %reduce-scatter.5.cloned.1.call-done = bf16[16,5120]{1,0:T(8,128)(2,1)} async-done(((bf16[128,5120]{1,0:T(8,128)(2,1)}), bf16[16,5120]{1,0:T(8,128)(2,1)}) %reduce-scatter.5.cloned.1.call-update) | async-done | bytes 163856 | tf_op jit(solution)/shard_map/reduce_scatter | solution.py:74
  (20 shorter events, 0.1 us)
Async XLA Ops:
  6.5 244.6 %all-gather.5.cloned.1.call-start = ((), (), s32[]{:S(2)}) async-start(), calls=%async_computation.3 | async-start | bytes 6389760 | tf_op jit(solution)/shard_map/all_gather | solution.py:56
  7.3 554.7 %all-gather.3.cloned.1.call-start = ((), (), s32[]{:S(2)}) async-start(), calls=%async_computation.2 | async-start | bytes 6389760 | tf_op jit(solution)/shard_map/all_gather | solution.py:55
  8.0 750.2 %reduce-scatter.3.cloned.1.call-start = ((), (), s32[]{:S(2)}) async-start(), calls=%async_computation.4 | async-start | bytes 884736 | tf_op jit(solution)/shard_map/reduce_scatter | solution.py:63
  569.4 3.6 copy-start
  580.6 3.6 copy-start
  592.2 3.6 copy-start
  603.9 3.6 copy-start
  684.2 121.1 %reduce-scatter.5.cloned.1.call-start = ((), (), s32[]{:S(2)}) async-start(), calls=%async_computation.5 | async-start | bytes 1474560 | tf_op jit(solution)/shard_map/reduce_scatter | solution.py:74
Sparse Core Ops, SparseCore 0:
  9.4 241.6 all-gather.4
  253.2 308.6 all-gather.2
  684.3 73.7 reduce-scatter.2
  763.3 41.9 reduce-scatter.4
where the time goes:
time: 812 us
  waiting for transfers between devices  618 us (76%)
  blocking collectives  111 us (14%)
  local copies, waits for them, and re-layouts  42.5 us (5%)
  matrix products  21.7 us (3%)
  between operations  13.2 us (2%)
    all_gather x1, waiting for transfers between devices, local(): lax.all_gather(key_vectors, 'ctx', axis=0, tiled=True)  303 us
    all_gather x1, waiting for transfers between devices, local(): lax.all_gather(value_vectors, 'ctx', axis=0, tiled=True)  224 us
    pmax x1, blocking collectives, local(): top_peak = lax.pmax(row_peak, 'tp')  66.1 us
    reduce_scatter x1, waiting for transfers between devices, local(): lax.psum_scatter(numerator.astype(jnp.bfloat16), 'tp', scatter_dimension=...  46.7 us
    reduce_scatter x1, waiting for transfers between devices, local(): lax.psum_scatter(jnp.dot(attended, out_weight, preferred_element_type=jnp...  42.1 us
    psum x1, blocking collectives, local(): all_totals = lax.psum(row_total * factor, 'tp')  27.2 us
    dynamic_slice x8, local copies, waits for them, and re-layouts, attend_piece(): finished, unused = lax.scan(absorb, running, (key_parts, value_parts))  26.1 us
    all_gather x1, blocking collectives, local(): all_queries = lax.all_gather(query_vectors, 'tp', axis=0, tiled=True)  17.3 us
  transfers between devices with their start and end apart: 4, of which 4 were waited for; matrix products, arithmetic and copies ran while one was open for 1% of the time, Pallas kernels for 0%

commit v1 on v0

--- a/solution.py
+++ b/solution.py
@@ -43,6 +43,18 @@
 
 
 def local(query_vectors, key_vectors, value_vectors, out_weight):
+
+    def put_windows_now(array_in):
+        return jnp.concatenate(
+            lax.all_to_all(
+                jnp.stack([array_in for _ in range(lax.axis_size("ctx"))]),
+                axis_name="ctx",
+                split_axis=0,
+                concat_axis=0,
+            ),
+            axis=0,
+        )
+
     score_scale = 1.0 / math.sqrt(HD)
     tp_count = lax.axis_size("tp")
     all_queries = lax.all_gather(query_vectors, "tp", axis=0, tiled=True)
@@ -52,7 +64,7 @@
     row_peak, row_total, weighted = attend_piece(
         fresh_state(row_count, head_count),
         query_heads,
-        lax.all_gather(key_vectors, "ctx", axis=0, tiled=True),
+        put_windows_now(key_vectors),
         lax.all_gather(value_vectors, "ctx", axis=0, tiled=True),
         score_scale,
     )

time: 812 us -> 591 us (0.73)
  the two profiles are of different devices: /device:TPU:21 before, /device:TPU:17 now
where the time goes in v1:
time: 591 us; the launch traced here: 590 us
  waiting for transfers between devices  302 us (51%)
  blocking collectives  185 us (31%)
  local copies, waits for them, and re-layouts  46.8 us (8%)
  matrix products  21.7 us (4%)
  starting transfers between devices  15 us (3%)
  between operations  13.2 us (2%)
    all_gather x1, waiting for transfers between devices, local(): lax.all_gather(value_vectors, 'ctx', axis=0, tiled=True)  188 us
    all_gather x1, blocking collectives, local(): all_queries = lax.all_gather(query_vectors, 'tp', axis=0, tiled=True)  97.2 us
    all_to_all x1, waiting for transfers between devices, put_windows_now(): lax.all_to_all(jnp.stack([array_in for _ in range(lax.axis_size('ctx'))])...  61.3 us
    pmax x1, blocking collectives, local(): top_peak = lax.pmax(row_peak, 'tp')  61 us
    reduce_scatter x1, waiting for transfers between devices, local(): lax.psum_scatter(jnp.dot(attended, out_weight, preferred_element_type=jnp...  41.7 us
    psum x1, blocking collectives, local(): all_totals = lax.psum(row_total * factor, 'tp')  27.2 us
    dynamic_slice x8, local copies, waits for them, and re-layouts, attend_piece(): finished, unused = lax.scan(absorb, running, (key_parts, value_parts))  26.1 us
    unnamed x5, local copies, waits for them, and re-layouts  16 us
  transfers between devices with their start and end apart: 4, of which 4 were waited for; matrix products, arithmetic and copies ran while one was open for 2% of the time, Pallas kernels for 0%

profile of v1, /device:TPU:17, one launch (start us, length us, event | category | flops | bytes accessed | tf_op | source)
XLA Modules:
  0.0 590.2 jit_solution(7567424278455338486)
XLA Ops:
  6.5 4.3 stack.2
  10.9 14.9 %all-to-all-start = ((bf16[64,16,3072]{2,1,0:T(8,128)(2,1)}), bf16[64,16,3072]{2,1,0:T(8,128)(2,1)}, u32[]{:S(2)}, u32[]{:S(2)}) async-start(bf16[64,16,3072]{2,1,0:T(8,128)(2,1)} %stack.2), calls=%async_computation | async-start | bytes 12582912 | tf_op jit(solution)/shard_map/all_to_all | solution.py:49
  25.8 0.0 all-gather.2.cloned.1.call-start
  25.8 0.7 all-gather.2.cloned.1.call-update
  26.5 0.0 reduce-scatter.3.cloned.1.call-start
  26.6 0.0 copy-done.1
  26.6 97.2 %all_gather.6 = bf16[128,3072]{1,0:T(8,128)(2,1)S(1)} all-gather(bf16[16,3072]{1,0:T(8,128)(2,1)S(1)} %copy-done.1), channel_id=1, replica_groups=mesh['ctx'=64,'tp'=8] {'tp'}, dimensions={0}, use_global_device_ids=true | all-gather | bytes 884736 | tf_op jit(solution)/shard_map/all_gather | solution.py:60
  123.8 0.4 copy.12
  124.2 1.2 copy.14
  125.4 61.3 %all-to-all-done = bf16[64,16,3072]{2,1,0:T(8,128)(2,1)} async-done(((bf16[64,16,3072]{2,1,0:T(8,128)(2,1)}), bf16[64,16,3072]{2,1,0:T(8,128)(2,1)}, u32[]{:S(2)}, u32[]{:S(2)}) %all-to-all-start) | async-done | bytes 6291488 | tf_op jit(solution)/shard_map/all_to_all | solution.py:49
  186.7 7.4 %copy.19 = bf16[128,8,24,128]{3,2,1,0:T(8,128)(2,1)} copy(bf16[128,8,24,128]{3,1,2,0:T(8,128)(2,1)} %bitcast.8) | data formatting | bytes 12582912
  194.1 187.9 %all-gather.2.cloned.1.call-done = bf16[1024,3072]{1,0:T(8,128)(2,1)} async-done(((bf16[16,3072]{1,0:T(8,128)(2,1)}), bf16[1024,3072]{1,0:T(8,128)(2,1)}) %all-gather.2.cloned.1.call-update) | async-done | bytes 6291472 | tf_op jit(solution)/shard_map/all_gather | solution.py:68
  382.0 7.4 %copy.20 = bf16[128,8,24,128]{3,2,1,0:T(8,128)(2,1)} copy(bf16[128,8,24,128]{3,1,2,0:T(8,128)(2,1)} %bitcast.54) | data formatting | bytes 12582912
  389.3 46.2 %while.15 = (s32[]{:T(128)}, f32[128,24]{0,1:T(8,128)S(1)}, f32[128,24]{0,1:T(8,128)S(1)}, f32[128,24,128]{0,2,1:T(8,128)}, bf16[4,256,24,128]{3,2,1,0:T(8,128)(...) while((s32[]{:T(128)}, f32[128,24]{0,1:T(8,128)S(1)}, ...), condition=%wide.region_3.4_spmd.clone, body=%wide.region_0.3_spmd.clone.sunk | while | flops 411712512 | bytes 29294728 | solution.py:41
  389.3 3.6 constant_dynamic-slice_fusion.4
  393.0 0.0 copy-done
  393.0 0.6 bitcast_reduce_fusion.2
  393.6 0.5 convert_reduce_fusion.2
  394.2 2.9 copy.28
  397.1 3.5 bitcast_add_fusion.2
  400.5 3.6 constant_dynamic-slice_fusion.4
  404.2 0.0 copy-done
  404.2 0.6 bitcast_reduce_fusion.2
  404.8 0.5 convert_reduce_fusion.2
  405.4 2.9 copy.28
  408.3 3.9 bitcast_add_fusion.2
  412.2 3.6 constant_dynamic-slice_fusion.4
  415.9 0.0 copy-done
  415.9 0.6 bitcast_reduce_fusion.2
  416.5 0.5 convert_reduce_fusion.2
  417.0 2.9 copy.28
  419.9 3.9 bitcast_add_fusion.2
  423.9 3.6 constant_dynamic-slice_fusion.4
  427.5 0.0 copy-done
  427.5 0.6 bitcast_reduce_fusion.2
  428.1 0.5 convert_reduce_fusion.2
  428.7 2.9 copy.28
  431.6 3.9 bitcast_add_fusion.2
  435.6 61.0 %pmax.7 = f32[128,24]{0,1:T(8,128)S(1)} all-reduce(f32[128,24]{0,1:T(8,128)S(1)} %get-tuple-element.45), channel_id=1, replica_groups=mesh['ctx'=64,'tp'=8] {'tp'}, use_global_device_ids=true, to_apply=%region_4.5 | all-reduce | flops 3072 | bytes 24576 | tf_op jit(solution)/shard_map/pmax | solution.py:71
  496.6 2.5 multiply_convert_fusion
  499.1 0.0 reduce-scatter.3.cloned.1.call-update
  499.1 0.0 reduce-scatter.5.cloned.1.call-start
  499.2 27.2 %psum.7 = f32[128,24]{0,1:T(8,128)S(1)} all-reduce(f32[128,24]{0,1:T(8,128)S(1)} %get-tuple-element.101), channel_id=1, replica_groups=mesh['ctx'=64,'tp'=8] {'tp'}, use_global_device_ids=true, to_apply=%region_6.7 | all-reduce | flops 3072 | bytes 24576 | tf_op jit(solution)/shard_map/psum | solution.py:73
  526.4 10.6 %reduce-scatter.3.cloned.1.call-done = bf16[128,384]{0,1:T(8,128)(2,1)} async-done(((bf16[128,3072]{0,1:T(8,128)(2,1)}), bf16[128,384]{0,1:T(8,128)(2,1)}) %reduce-scatter.3.cloned.1.call-update) | async-done | bytes 98320 | tf_op jit(solution)/shard_map/reduce_scatter | solution.py:75
  537.0 0.9 fusion.10
  537.9 4.1 convolution_convert_fusion
  542.0 0.0 reduce-scatter.5.cloned.1.call-update
  542.0 41.7 %reduce-scatter.5.cloned.1.call-done = bf16[16,5120]{1,0:T(8,128)(2,1)} async-done(((bf16[128,5120]{1,0:T(8,128)(2,1)}), bf16[16,5120]{1,0:T(8,128)(2,1)}) %reduce-scatter.5.cloned.1.call-update) | async-done | bytes 163856 | tf_op jit(solution)/shard_map/reduce_scatter | solution.py:86
  (22 shorter events, 0.1 us)
Async XLA Ops:
  10.9 15.7 %copy-start.1 = (bf16[16,3072]{1,0:T(8,128)(2,1)S(1)}, bf16[16,3072]{1,0:T(8,128)(2,1)}, u32[]{:S(2)}) copy-start(bf16[16,3072]{1,0:T(8,128)(2,1)} %param.6) | copy-start | bytes 294916
  10.9 175.8 %all-to-all-start = ((bf16[64,16,3072]{2,1,0:T(8,128)(2,1)}), bf16[64,16,3072]{2,1,0:T(8,128)(2,1)}, u32[]{:S(2)}, u32[]{:S(2)}) async-start(bf16[64,16,3072]{2,1,0:T(8,128)(2,1)} %stack.2), calls=%async_computation | async-start | bytes 12582912 | tf_op jit(solution)/shard_map/all_to_all | solution.py:49
  25.8 356.2 %all-gather.2.cloned.1.call-start = ((), (), s32[]{:S(2)}) async-start(), calls=%async_computation.3 | async-start | bytes 6389760 | tf_op jit(solution)/shard_map/all_gather | solution.py:68
  26.5 510.5 %reduce-scatter.3.cloned.1.call-start = ((), (), s32[]{:S(2)}) async-start(), calls=%async_computation.4 | async-start | bytes 884736 | tf_op jit(solution)/shard_map/reduce_scatter | solution.py:75
  389.3 3.6 copy-start
  400.5 3.6 copy-start
  412.2 3.6 copy-start
  423.9 3.6 copy-start
  499.1 84.5 %reduce-scatter.5.cloned.1.call-start = ((), (), s32[]{:S(2)}) async-start(), calls=%async_computation.5 | async-start | bytes 1474560 | tf_op jit(solution)/shard_map/reduce_scatter | solution.py:86
Sparse Core Ops, SparseCore 0:
  28.7 353.2 all-gather.1
  499.3 37.6 reduce-scatter.2
  542.1 41.5 reduce-scatter.4
